TPU v7x, 32 devices: a whole 2x2x4 slice. The times are simulated.
32 devices in a mesh: gx: 4 (over y, x), gy: 8 (over z, core).
Axes of the slice: x: 2, y: 2, z: 4, core: 2. Of those that a mesh axis runs over, the one named last changes fastest.
Arguments:
- right_side: float32 [8, 3, 64, 1024], P(None, None, 'gx', 'gy'), may hold values from -50 to 50
- first_guess: float32 [8, 3, 64, 1024], P(None, None, 'gx', 'gy'), may hold values from -3 to 3
- diag_block: bfloat16 [8, 3, 3, 64, 1024], P(None, None, None, 'gx', 'gy'), may hold values from -2.41 to 12
- mobility: bfloat16 [8, 3, 3, 64, 1024], P(None, None, None, 'gx', 'gy'), may hold values from -1 to 1.21
- face_trans: bfloat16 [6, 8, 64, 1024], P(None, None, 'gx', 'gy'), may hold values from 0.19921875 to 1
- column_inverse: bfloat16 [4, 6, 6, 64, 1024], P(None, None, None, 'gx', 'gy'), may hold values from -0.061 to 0.201
- perf_cell: int32 [32, 32, 40], P(('gx', 'gy')), may hold values from 0 to 16383, as said below
- perf_slot: int32 [32, 32, 40], P(('gx', 'gy')), may hold values from 0 to 1024, as said below
- well_in: float32 [3, 32768], P(None, ('gx', 'gy')), may hold values from -4 to 4
- well_out: float32 [3, 32768], P(None, ('gx', 'gy')), may hold values from -4 to 4
- well_inverse: float32 [256, 128, 128], P(('gx', 'gy')), may hold values from -1 to 1
Outputs:
- solution: float32 [8, 3, 64, 1024], P(None, None, 'gx', 'gy')
- residual: float32 [8, 3, 64, 1024], P(None, None, 'gx', 'gy')
Inputs may be any that keep to these rules, and one draw needn't show every extreme that they name: `perf_cell`: entry [s, d, q] is a local cell number of device s's tile, the cell of slot q from device s to owner d; the slot's segment is perf_slot[d, s, q]; slots that perf_slot marks empty carry an arbitrary cell. `perf_slot`: entry [d, s, q] is w * 128 + g when slot q from device s carries segment g of owner d's local well w, and 1024 when the slot is empty. Each segment of an owner appears at most once; the segments of a well that appear are 0 to n - 1 for its padded count n of 1 to 128. Every pair (d, s) has at most 40 live slots and some pair has exactly 40; in every draw some owner has all 1024 segments live.
All inputs are finite; a program needn't handle non-finite values.
Results may differ from a plain program's by a relative error of at most 0.0003.
Values sent between devices are 32-bit elements; how exact they have to be, the bound alone decides.
No kernel may reach another device: no remote copies, remote signals or barrier semaphores. Data moves between devices by JAX's collectives and lax.ppermute only.
A program may use at most 128 MiB of HBM per device.

v0:
```python
import jax
import jax.numpy as jnp
from jax import lax
from jax.sharding import PartitionSpec as P

ITERS = 2


def padded_2(block, sides, width):
    for axis, dim in sides:
        count = lax.axis_size(axis)
        forward = [(i, i + 1) for i in range(count - 1)]
        backward = [(target, source) for source, target in forward]
        low = lax.ppermute(
            lax.slice_in_dim(block, block.shape[dim] - width, None, axis=dim), axis, forward
        )
        high = lax.ppermute(lax.slice_in_dim(block, 0, width, axis=dim), axis, backward)
        block = jnp.concatenate([low, block, high], axis=dim)
    return block


def couple(mixing, vector):
    summed = mixing[:, :, 0].astype(jnp.float32) * vector[:, 0:1]
    summed = summed + mixing[:, :, 1].astype(jnp.float32) * vector[:, 1:2]
    summed = summed + mixing[:, :, 2].astype(jnp.float32) * vector[:, 2:3]
    return summed


def stencil(vector, extended, diag_block, face_trans):
    factor = face_trans.astype(jnp.float32)[:, :, None]
    interior = extended[:, :, 1:-1, 1:-1]
    zero_layer = jnp.zeros_like(interior[:1])
    under_layer = jnp.concatenate([zero_layer, interior[:-1]], axis=0)
    over_layer = jnp.concatenate([interior[1:], zero_layer], axis=0)
    beside = factor[0] * extended[:, :, :-2, 1:-1]
    beside = beside + factor[1] * extended[:, :, 2:, 1:-1]
    beside = beside + factor[2] * extended[:, :, 1:-1, :-2]
    beside = beside + factor[3] * extended[:, :, 1:-1, 2:]
    beside = beside + factor[4] * under_layer
    beside = beside + factor[5] * over_layer
    return couple(diag_block, vector) - beside


def precondition(vector, column_inverse):
    layers, comps, tile_rows, tile_cols = vector.shape
    paired = vector.reshape(layers // 2, 6, tile_rows, tile_cols)
    result = column_inverse[:, :, 0].astype(jnp.float32) * paired[:, 0:1]
    for member in range(1, 6):
        result = (
            result
            + column_inverse[:, :, member].astype(jnp.float32) * paired[:, member : member + 1]
        )
    return result.reshape(vector.shape)


def per_device(
    right_side,
    first_guess,
    diag_block,
    mobility,
    face_trans,
    column_inverse,
    perf_cell,
    perf_slot,
    well_in,
    well_out,
    well_inverse,
):
    layers, comps, tile_rows, tile_cols = right_side.shape
    tile_area = tile_rows * tile_cols
    cell_ids = perf_cell[0]
    targets = perf_slot[0]
    layer_idx = cell_ids // tile_area
    column_idx = cell_ids % tile_area
    well_count = well_inverse.shape[0]
    seg_count = well_inverse.shape[1]
    per_owner = well_count * seg_count
    pad_in = jnp.concatenate([well_in, jnp.zeros((3, 1), jnp.float32)], axis=1)
    pad_out = jnp.concatenate([well_out, jnp.zeros((3, 1), jnp.float32)], axis=1)

    def solve_wells(rate):
        totals = jnp.zeros((per_owner + 1,), jnp.float32).at[targets].add(rate)
        seg_rate = jnp.einsum(
            "wgh,wh->wg",
            well_inverse,
            totals[:per_owner].reshape(well_count, seg_count),
            precision=lax.Precision.HIGHEST,
        )
        padded = jnp.concatenate([seg_rate.reshape(-1), jnp.zeros((1,), jnp.float32)])
        return padded[targets]

    def well_term(vector):
        flattened = vector.reshape(layers, comps, tile_area)
        values = flattened[layer_idx, :, column_idx]
        outgoing = jnp.moveaxis(values, 2, 0)
        arrived = lax.all_to_all(outgoing, ("gx", "gy"), split_axis=1, concat_axis=1, tiled=True)
        coeff_in = pad_in[:, targets]
        rate = coeff_in[0] * arrived[0] + coeff_in[1] * arrived[1] + coeff_in[2] * arrived[2]
        back = solve_wells(rate)
        terms = lax.all_to_all(
            pad_out[:, targets] * back[None], ("gx", "gy"), split_axis=1, concat_axis=1, tiled=True
        )
        scattered = (
            jnp.zeros((layers, comps, tile_area), jnp.float32)
            .at[layer_idx, :, column_idx]
            .add(jnp.moveaxis(terms, 0, 2))
        )
        return scattered.reshape(vector.shape)

    def apply_operator(vector):
        flux = couple(mobility, vector)
        extended = padded_2(flux, (("gx", 2), ("gy", 3)), 1)
        return stencil(vector, extended, diag_block, face_trans) - well_term(vector)

    iterate = first_guess
    residual = right_side - apply_operator(iterate)
    shadow = residual
    inner_now = lax.psum(jnp.sum(shadow * residual), ("gx", "gy"))
    search = residual
    for iteration in range(ITERS):
        search_hat = precondition(search, column_inverse)
        applied = apply_operator(search_hat)
        projected = lax.psum(jnp.sum(shadow * applied), ("gx", "gy"))
        step_size = inner_now / projected
        halfway = residual - step_size * applied
        halfway_hat = precondition(halfway, column_inverse)
        response = apply_operator(halfway_hat)
        cross_term, self_term, shadow_term = lax.psum(
            (jnp.sum(response * halfway), jnp.sum(response * response), jnp.sum(shadow * response)),
            ("gx", "gy"),
        )
        smoothing = cross_term / self_term
        iterate = iterate + step_size * search_hat + smoothing * halfway_hat
        residual = halfway - smoothing * response
        if iteration + 1 < ITERS:
            inner_next = inner_now - step_size * projected - smoothing * shadow_term
            momentum = inner_next / inner_now * (step_size / smoothing)
            search = residual + momentum * (search - smoothing * applied)
            inner_now = inner_next
    return (iterate, right_side - apply_operator(iterate))


def solution(mesh):
    in_specs = (
        P(None, None, "gx", "gy"),
        P(None, None, "gx", "gy"),
        P(None, None, None, "gx", "gy"),
        P(None, None, None, "gx", "gy"),
        P(None, None, "gx", "gy"),
        P(None, None, None, "gx", "gy"),
        P(("gx", "gy"), None, None),
        P(("gx", "gy"), None, None),
        P(None, ("gx", "gy")),
        P(None, ("gx", "gy")),
        P(("gx", "gy"), None, None),
    )
    out_specs = (P(None, None, "gx", "gy"), P(None, None, "gx", "gy"))
    return jax.shard_map(
        per_device, mesh=mesh, in_specs=in_specs, out_specs=out_specs, check_vma=False
    )
```

profile of v0, /device:TPU:0, one launch (start us, length us, event | category | flops | bytes accessed | tf_op | source)
XLA Modules:
  0.0 751.7 jit_solution(8360309148296932770)
XLA Ops:
  1.6 5.7 copy.372
  7.4 9.6 %gather_fusion.2 = f32[1280,3]{1,0:T(8,128)S(1)} fusion(f32[8,3,2048]{1,2,0:T(8,128)} %bitcast.585, s32[1280]{0:T(1024)S(1)} %reshape.496), kind=kCustom, calls=%fused_computation.2 | custom fusion | bytes 40960 | tf_op jit(solution)/shard_map/gather | solution.py:94
  17.8 7.3 all-to-all-start
  26.7 4.5 collective-permute-start
  45.9 3.8 collective-permute-start.2
  49.9 7.3 scatter_custom_fusion
  58.2 7.1 gather_fusion.3
  66.1 6.4 all-to-all-start.1
  73.1 6.7 all-to-all-done.1
  81.0 13.1 %scatter_custom_fusion.6 = f32[3,16384]{0,1:T(8,128)} fusion(s32[1280]{0:T(1024)S(1)} %reshape.628, f32[1280,3]{1,0:T(8,128)} %bitcast.636, f32[]{:T(128)} %constant.32.clone.1), kind=kCustom, calls=%fused_computation.36 | custom fusion | flops 3840 | bytes 197120
  94.2 5.9 copy.377
  106.4 5.1 collective-permute-start.4
  113.1 5.6 copy.398
  118.7 12.7 %gather_fusion.4 = f32[1280,3]{1,0:T(8,128)} fusion(f32[8,3,2048]{1,2,0:T(8,128)} %copy.398, s32[1280]{0:T(1024)S(1)} %reshape.496), kind=kCustom, calls=%fused_computation.4 | custom fusion | bytes 40960 | tf_op jit(solution)/shard_map/gather | solution.py:94
  147.1 7.5 scatter_custom_fusion.1
  155.5 10.0 %gather_fusion.5 = f32[1280]{0:T(1024)} fusion(f32[1025]{0:T(1024)S(1)} %pad_maximum_fusion.58, s32[2048]{0:T(1024)} %copy-done.22), kind=kCustom, calls=%fused_computation.5 | custom fusion | bytes 15360 | tf_op jit(solution)/shard_map/gather | solution.py:90
  168.4 6.0 all-to-all-start.3
  176.1 5.6 all-to-all-done.3
  183.7 12.9 %scatter_custom_fusion.7 = f32[3,16384]{0,1:T(8,128)} fusion(s32[1280]{0:T(1024)} %copy-done.70, f32[1280,3]{1,0:T(8,128)} %bitcast.637, f32[]{:T(128)} %constant.32.clone.1), kind=kCustom, calls=%fused_computation.34 | custom fusion | flops 3840 | bytes 197120
  196.6 5.9 copy.403
  206.1 38.8 %all-reduce.16 = (f32[]{:T(128)}, f32[]{:T(128)}) all-reduce(f32[]{:T(128)} %get-tuple-element.18, f32[]{:T(128)} %get-tuple-element.17), channel_id=1, replica_groups=mesh['gx'=4,'gy'=8] {'gx','gy'}, use_global_device_ids=true, to_apply=%region_3.4 | all-reduce | flops 2 | bytes 16 | tf_op jit(solution)/shard_map/psum | solution.py:118
  252.2 5.4 collective-permute-start.8
  258.9 5.6 copy.418
  264.5 12.7 %gather_fusion.6 = f32[1280,3]{1,0:T(8,128)} fusion(f32[8,3,2048]{1,2,0:T(8,128)} %copy.418, s32[1280]{0:T(1024)S(1)} %reshape.496), kind=kCustom, calls=%fused_computation.6 | custom fusion | bytes 40960 | tf_op jit(solution)/shard_map/gather | solution.py:94
  279.2 4.0 all-to-all-start.4
  293.6 7.5 scatter_custom_fusion.2
  302.0 10.0 %gather_fusion.7 = f32[1280]{0:T(1024)} fusion(f32[1025]{0:T(1024)S(1)} %pad_maximum_fusion.57, s32[2048]{0:T(1024)} %copy-done.22), kind=kCustom, calls=%fused_computation.7 | custom fusion | bytes 15360 | tf_op jit(solution)/shard_map/gather | solution.py:90
  314.9 6.0 all-to-all-start.5
  323.9 4.1 all-to-all-done.5
  330.1 12.9 %scatter_custom_fusion.8 = f32[3,16384]{0,1:T(8,128)} fusion(s32[1280]{0:T(1024)} %copy-done.70, f32[1280,3]{1,0:T(8,128)} %bitcast.638, f32[]{:T(128)} %constant.32.clone.1), kind=kCustom, calls=%fused_computation.32 | custom fusion | flops 3840 | bytes 197120
  343.0 5.9 copy.423
  352.5 38.6 %all-reduce.15 = (f32[]{:T(128)}, f32[]{:T(128)}, f32[]{:T(128)}) all-reduce(f32[]{:T(128)} %get-tuple-element.16, f32[]{:T(128)} %get-tuple-element.15, f32[]{:T(128)} %get-tuple-element.14), channel_id=1, replica_groups=mesh['gx'=4,'gy'=8] {'gx','gy'}, use_global_device_ids=true, to_apply=%region_11.12 | all-reduce | flops 3 | bytes 24 | tf_op jit(solution)/shard_map/psum | solution.py:128
  401.7 5.4 collective-permute-start.12
  408.5 5.6 copy.437
  414.1 12.7 %gather_fusion.8 = f32[1280,3]{1,0:T(8,128)} fusion(f32[8,3,2048]{1,2,0:T(8,128)} %copy.437, s32[1280]{0:T(1024)S(1)} %reshape.496), kind=kCustom, calls=%fused_computation.8 | custom fusion | bytes 40960 | tf_op jit(solution)/shard_map/gather | solution.py:94
  428.8 3.9 all-to-all-start.6
  443.0 7.5 scatter_custom_fusion.3
  451.5 10.0 %gather_fusion.9 = f32[1280]{0:T(1024)} fusion(f32[1025]{0:T(1024)S(1)} %pad_maximum_fusion.56, s32[2048]{0:T(1024)} %copy-done.22), kind=kCustom, calls=%fused_computation.9 | custom fusion | bytes 15360 | tf_op jit(solution)/shard_map/gather | solution.py:90
  464.3 6.0 all-to-all-start.7
  472.1 5.6 all-to-all-done.7
  479.7 12.9 %scatter_custom_fusion.9 = f32[3,16384]{0,1:T(8,128)} fusion(s32[1280]{0:T(1024)} %copy-done.70, f32[1280,3]{1,0:T(8,128)} %bitcast.639, f32[]{:T(128)} %constant.32.clone.1), kind=kCustom, calls=%fused_computation.30 | custom fusion | flops 3840 | bytes 197120
  492.6 5.9 copy.442
  501.9 38.4 %psum.61 = f32[]{:T(128)} all-reduce(f32[]{:T(128)} %get-tuple-element.26), channel_id=1, replica_groups=mesh['gx'=4,'gy'=8] {'gx','gy'}, use_global_device_ids=true, to_apply=%region_19.20 | all-reduce | flops 1 | bytes 8 | tf_op jit(solution)/shard_map/psum | solution.py:123
  545.6 4.8 collective-permute-start.16
  551.2 4.7 copy.456
  555.9 9.6 %gather_fusion.10 = f32[1280,3]{1,0:T(8,128)S(1)} fusion(f32[8,3,2048]{1,2,0:T(8,128)} %copy.456, s32[1280]{0:T(1024)S(1)} %reshape.496), kind=kCustom, calls=%fused_computation.10 | custom fusion | bytes 40960 | tf_op jit(solution)/shard_map/gather | solution.py:94
  566.4 4.4 all-to-all-start.8
  578.3 7.5 scatter_custom_fusion.4
  586.8 7.1 gather_fusion.11
  594.6 4.8 all-to-all-start.9
  600.2 6.7 all-to-all-done.9
  608.2 12.9 %scatter_custom_fusion.10 = f32[3,16384]{0,1:T(8,128)} fusion(s32[1280]{0:T(1024)} %copy-done.70, f32[1280,3]{1,0:T(8,128)} %bitcast.640, f32[]{:T(128)} %constant.32.clone.1), kind=kCustom, calls=%fused_computation.28 | custom fusion | flops 3840 | bytes 197120
  621.1 5.3 copy.461
  628.7 38.6 %all-reduce.14 = (f32[]{:T(128)}, f32[]{:T(128)}) all-reduce(f32[]{:T(128)} %get-tuple-element.13, f32[]{:T(128)} %get-tuple-element.12), channel_id=1, replica_groups=mesh['gx'=4,'gy'=8] {'gx','gy'}, use_global_device_ids=true, to_apply=%region_23.24 | all-reduce | flops 2 | bytes 16 | tf_op jit(solution)/shard_map/psum | solution.py:128
  670.3 4.8 collective-permute-start.20
  675.1 4.7 copy.462
  679.7 9.6 %gather_fusion.12 = f32[1280,3]{1,0:T(8,128)S(1)} fusion(f32[8,3,2048]{1,2,0:T(8,128)} %bitcast.586, s32[1280]{0:T(1024)S(1)} %reshape.496), kind=kCustom, calls=%fused_computation.12 | custom fusion | bytes 40960 | tf_op jit(solution)/shard_map/gather | solution.py:94
  690.2 4.4 all-to-all-start.10
  702.2 7.5 scatter_custom_fusion.5
  710.7 7.1 gather_fusion.13
  718.5 4.8 all-to-all-start.11
  724.0 6.7 all-to-all-done.11
  731.0 12.8 %scatter_custom_fusion.11 = f32[3,16384]{0,1:T(8,128)} fusion(s32[1280]{0:T(1024)} %copy-done.70, f32[1280,3]{1,0:T(8,128)S(1)} %bitcast.635, f32[]{:T(128)} %constant.32.clone.1), kind=kCustom, calls=%fused_computation.26 | custom fusion | flops 3840 | bytes 197120
  743.8 5.2 copy.467
  (385 shorter events, 150.4 us)
Async XLA Ops:
  0.6 56.6 %copy-start = (f32[8,128,128]{2,1,0:T(8,128)S(1)}, f32[8,128,128]{2,1,0:T(8,128)}, u32[]{:S(2)}) copy-start(f32[8,128,128]{2,1,0:T(8,128)} %param.21) | copy-start | bytes 1572868
  0.6 24.5 %copy-start.36 = (f32[8,3,16,128]{3,2,1,0:T(8,128)S(1)}, f32[8,3,16,128]{3,2,1,0:T(8,128)}, u32[]{:S(2)}) copy-start(f32[8,3,16,128]{3,2,1,0:T(8,128)} %param.12) | copy-start | bytes 589828
  0.7 24.5 %copy-start.57 = (bf16[8,3,3,16,128]{4,3,2,1,0:T(8,128)(2,1)S(1)}, bf16[8,3,3,16,128]{4,3,2,1,0:T(8,128)(2,1)}, u32[]{:S(2)}) copy-start(bf16[8,3,3,16,128]{4,3,2,1,0:T(8,128)(2,1)} %param.14) | copy-start | bytes 884740
  1.5 30.6 %copy-start.39 = (bf16[4,6,6,16,128]{4,3,2,1,0:T(8,128)(2,1)S(1)}, bf16[4,6,6,16,128]{4,3,2,1,0:T(8,128)(2,1)}, u32[]{:S(2)}) copy-start(bf16[4,6,6,16,128]{4,3,2,1,0:T(8,128)(2,1)} %param.16) | copy-start | bytes 1769476
  1.5 30.7 %copy-start.71 = (s32[2]{0:T(128)S(1)}, s32[2]{0:T(128)}, u32[]{:S(2)}) copy-start(s32[2]{0:T(128)} %constant.76) | copy-start | bytes 28
  1.5 30.8 %copy-start.72 = (s32[2]{0:T(128)S(1)}, s32[2]{0:T(128)}, u32[]{:S(2)}) copy-start(s32[2]{0:T(128)} %constant.73) | copy-start | bytes 28
  1.5 30.8 %copy-start.69 = (s32[1,32,40]{2,1,0:T(8,128)S(1)}, s32[1,32,40]{2,1,0:T(8,128)}, u32[]{:S(2)}) copy-start(s32[1,32,40]{2,1,0:T(8,128)} %param.18) | copy-start | bytes 15364
  1.5 30.9 %copy-start.59 = (bf16[6,8,16,128]{3,2,1,0:T(8,128)(2,1)S(1)}, bf16[6,8,16,128]{3,2,1,0:T(8,128)(2,1)}, u32[]{:S(2)}) copy-start(bf16[6,8,16,128]{3,2,1,0:T(8,128)(2,1)} %param.15) | copy-start | bytes 589828
  7.3 26.0 %copy-start.58 = (bf16[8,3,3,16,128]{4,3,2,1,0:T(8,128)(2,1)S(1)}, bf16[8,3,3,16,128]{4,3,2,1,0:T(8,128)(2,1)}, u32[]{:S(2)}) copy-start(bf16[8,3,3,16,128]{4,3,2,1,0:T(8,128)(2,1)} %param.13) | copy-start | bytes 884740
  7.3 26.8 %copy-start.67 = (f32[3,1024]{1,0:T(4,128)S(1)}, f32[3,1024]{1,0:T(4,128)}, u32[]{:S(2)}) copy-start(f32[3,1024]{1,0:T(4,128)} %param.20) | copy-start | bytes 36868
  7.3 31.5 %copy-start.68 = (f32[3,1024]{1,0:T(4,128)S(1)}, f32[3,1024]{1,0:T(4,128)}, u32[]{:S(2)}) copy-start(f32[3,1024]{1,0:T(4,128)} %param.19) | copy-start | bytes 36868
  17.8 31.9 %all-to-all-start = ((f32[3,32,40]{2,0,1:T(4,128)}), f32[3,32,40]{2,0,1:T(4,128)S(1)}, u32[]{:S(2)}, u32[]{:S(2)}) async-start(f32[3,32,40]{2,0,1:T(4,128)} %bitcast.22), calls=%async_computation | async-start | bytes 131072 | tf_op jit(solution)/shard_map/all_to_all | solution.py:96
  25.4 32.8 %copy-start.11 = (f32[8,3,16,128]{3,2,0,1:T(8,128)}, f32[8,3,16,128]{3,2,0,1:T(8,128)S(1)}, u32[]{:S(2)}) copy-start(f32[8,3,16,128]{3,2,0,1:T(8,128)S(1)} %fusion.39) | copy-start | bytes 589828
  25.4 18.2 %collective-permute-start.1 = (f32[8,3,1,128]{3,2,0,1:T(1,128)S(1)}, f32[8,3,1,128]{3,2,0,1:T(1,128)S(1)}, u32[]{:S(2)}, u32[]{:S(2)}) collective-permute-start(f32[8,3,1,128]{3,2,0,1:T(1,128)S(1)} %get-tuple-element.122), channel_id=1, source_target_pairs={{8,0},{16,8},{24,16},{9,1},{17,9},{25,17},{10,2},{18,10},{26,18},{... | collective-permute-start | bytes 36872 | tf_op jit(solution)/shard_map/ppermute | solution.py:17
  26.7 16.9 %collective-permute-start = (f32[8,3,1,128]{3,2,0,1:T(1,128)S(1)}, f32[8,3,1,128]{3,2,0,1:T(1,128)S(1)}, u32[]{:S(2)}, u32[]{:S(2)}) collective-permute-start(f32[8,3,1,128]{3,2,0,1:T(1,128)S(1)} %get-tuple-element.121), channel_id=1, source_target_pairs={{0,8},{8,16},{16,24},{1,9},{9,17},{17,25},{2,10},{10,18},{18,26},{... | collective-permute-start | bytes 36872 | tf_op jit(solution)/shard_map/ppermute | solution.py:14
  32.5 32.8 %copy-start.66 = (s32[1280]{0:T(1024)}, s32[1280]{0:T(1024)S(1)}, u32[]{:S(2)}) copy-start(s32[1280]{0:T(1024)S(1)} %reshape.482) | copy-start | bytes 15364
  34.0 31.3 %copy-start.22 = (s32[2048]{0:T(1024)}, s32[2048]{0:T(1024)S(1)}, u32[]{:S(2)}) copy-start(s32[2048]{0:T(1024)S(1)} %pad_clamp_fusion) | copy-start | bytes 24580
  38.8 26.6 %copy-start.20 = (f32[32,40,3]{1,2,0:T(4,128)}, f32[32,40,3]{1,2,0:T(4,128)S(1)}, u32[]{:S(2)}) copy-start(f32[32,40,3]{1,2,0:T(4,128)S(1)} %copy.374) | copy-start | bytes 46084
  44.6 55.5 %collective-permute-start.3 = (f32[8,3,18,1]{3,2,0,1:T(8,128)}, f32[8,3,18,1]{3,2,0,1:T(8,128)}, u32[]{:S(2)}, u32[]{:S(2)}) collective-permute-start(f32[8,3,18,1]{3,2,0,1:T(8,128)} %get-tuple-element.56), channel_id=1, source_target_pairs={{1,0},{2,1},{3,2},{4,3},{5,4},{6,5},{7,6},{9,8},{10,9},{11,10},{12... | collective-permute-start | bytes 5192 | tf_op jit(solution)/shard_map/ppermute | solution.py:17
  45.9 54.2 %collective-permute-start.2 = (f32[8,3,18,1]{3,2,0,1:T(8,128)}, f32[8,3,18,1]{3,2,0,1:T(8,128)}, u32[]{:S(2)}, u32[]{:S(2)}) collective-permute-start(f32[8,3,18,1]{3,2,0,1:T(8,128)} %get-tuple-element.55), channel_id=1, source_target_pairs={{0,1},{1,2},{2,3},{3,4},{4,5},{5,6},{6,7},{8,9},{9,10},{10,11},{11... | collective-permute-start | bytes 5192 | tf_op jit(solution)/shard_map/ppermute | solution.py:14
  66.1 13.8 %all-to-all-start.1 = ((f32[3,32,40]{2,0,1:T(4,128)}), f32[3,32,40]{2,0,1:T(4,128)S(1)}, u32[]{:S(2)}, u32[]{:S(2)}) async-start(f32[3,32,40]{2,0,1:T(4,128)} %multiply_bitcast_fusion.5), calls=%async_computation.1 | async-start | bytes 131072 | tf_op jit(solution)/shard_map/all_to_all | solution.py:100
  72.6 27.5 %copy-start.70 = (s32[1280]{0:T(1024)}, s32[1280]{0:T(1024)S(1)}, u32[]{:S(2)}) copy-start(s32[1280]{0:T(1024)S(1)} %reshape.628) | copy-start | bytes 15364
  105.1 31.6 %collective-permute-start.5 = (f32[8,3,1,128]{3,2,0,1:T(1,128)}, f32[8,3,1,128]{3,2,0,1:T(1,128)}, u32[]{:S(2)}, u32[]{:S(2)}) collective-permute-start(f32[8,3,1,128]{3,2,0,1:T(1,128)} %get-tuple-element.107), channel_id=1, source_target_pairs={{8,0},{16,8},{24,16},{9,1},{17,9},{25,17},{10,2},{18,10},{26,18},{... | collective-permute-start | bytes 36872 | tf_op jit(solution)/shard_map/ppermute | solution.py:17
  106.4 30.3 %collective-permute-start.4 = (f32[8,3,1,128]{3,2,0,1:T(1,128)}, f32[8,3,1,128]{3,2,0,1:T(1,128)}, u32[]{:S(2)}, u32[]{:S(2)}) collective-permute-start(f32[8,3,1,128]{3,2,0,1:T(1,128)} %get-tuple-element.106), channel_id=1, source_target_pairs={{0,8},{8,16},{16,24},{1,9},{9,17},{17,25},{2,10},{10,18},{18,26},{... | collective-permute-start | bytes 36872 | tf_op jit(solution)/shard_map/ppermute | solution.py:14
  133.4 10.5 %all-to-all-start.2 = ((f32[3,32,40]{2,0,1:T(4,128)}), f32[3,32,40]{2,0,1:T(4,128)}, u32[]{:S(2)}, u32[]{:S(2)}) async-start(f32[3,32,40]{2,0,1:T(4,128)} %bitcast.707), calls=%async_computation.2 | async-start | bytes 131072 | tf_op jit(solution)/shard_map/all_to_all | solution.py:96
  138.6 63.9 %collective-permute-start.7 = (f32[8,3,18,1]{3,2,0,1:T(8,128)}, f32[8,3,18,1]{3,2,0,1:T(8,128)}, u32[]{:S(2)}, u32[]{:S(2)}) collective-permute-start(f32[8,3,18,1]{3,2,0,1:T(8,128)} %get-tuple-element.51), channel_id=1, source_target_pairs={{1,0},{2,1},{3,2},{4,3},{5,4},{6,5},{7,6},{9,8},{10,9},{11,10},{12... | collective-permute-start | bytes 5192 | tf_op jit(solution)/shard_map/ppermute | solution.py:17
  139.9 62.6 %collective-permute-start.6 = (f32[8,3,18,1]{3,2,0,1:T(8,128)}, f32[8,3,18,1]{3,2,0,1:T(8,128)}, u32[]{:S(2)}, u32[]{:S(2)}) collective-permute-start(f32[8,3,18,1]{3,2,0,1:T(8,128)} %get-tuple-element.50), channel_id=1, source_target_pairs={{0,1},{1,2},{2,3},{3,4},{4,5},{5,6},{6,7},{8,9},{9,10},{10,11},{11... | collective-permute-start | bytes 5192 | tf_op jit(solution)/shard_map/ppermute | solution.py:14
  168.4 13.3 %all-to-all-start.3 = ((f32[3,32,40]{2,0,1:T(4,128)}), f32[3,32,40]{2,0,1:T(4,128)}, u32[]{:S(2)}, u32[]{:S(2)}) async-start(f32[3,32,40]{2,0,1:T(4,128)} %multiply_bitcast_fusion.4), calls=%async_computation.3 | async-start | bytes 131072 | tf_op jit(solution)/shard_map/all_to_all | solution.py:100
  250.8 32.3 %collective-permute-start.9 = (f32[8,3,1,128]{3,2,0,1:T(1,128)}, f32[8,3,1,128]{3,2,0,1:T(1,128)}, u32[]{:S(2)}, u32[]{:S(2)}) collective-permute-start(f32[8,3,1,128]{3,2,0,1:T(1,128)} %get-tuple-element.94), channel_id=1, source_target_pairs={{8,0},{16,8},{24,16},{9,1},{17,9},{25,17},{10,2},{18,10},{26,18},{... | collective-permute-start | bytes 36872 | tf_op jit(solution)/shard_map/ppermute | solution.py:17
  252.2 31.0 %collective-permute-start.8 = (f32[8,3,1,128]{3,2,0,1:T(1,128)}, f32[8,3,1,128]{3,2,0,1:T(1,128)}, u32[]{:S(2)}, u32[]{:S(2)}) collective-permute-start(f32[8,3,1,128]{3,2,0,1:T(1,128)} %get-tuple-element.93), channel_id=1, source_target_pairs={{0,8},{8,16},{16,24},{1,9},{9,17},{17,25},{2,10},{10,18},{18,26},{... | collective-permute-start | bytes 36872 | tf_op jit(solution)/shard_map/ppermute | solution.py:14
  279.2 11.2 %all-to-all-start.4 = ((f32[3,32,40]{2,0,1:T(4,128)}), f32[3,32,40]{2,0,1:T(4,128)}, u32[]{:S(2)}, u32[]{:S(2)}) async-start(f32[3,32,40]{2,0,1:T(4,128)} %bitcast.708), calls=%async_computation.4 | async-start | bytes 131072 | tf_op jit(solution)/shard_map/all_to_all | solution.py:96
  285.1 63.8 %collective-permute-start.11 = (f32[8,3,18,1]{3,2,0,1:T(8,128)}, f32[8,3,18,1]{3,2,0,1:T(8,128)}, u32[]{:S(2)}, u32[]{:S(2)}) collective-permute-start(f32[8,3,18,1]{3,2,0,1:T(8,128)} %get-tuple-element.49), channel_id=1, source_target_pairs={{1,0},{2,1},{3,2},{4,3},{5,4},{6,5},{7,6},{9,8},{10,9},{11,10},{12... | collective-permute-start | bytes 5192 | tf_op jit(solution)/shard_map/ppermute | solution.py:17
  286.4 62.5 %collective-permute-start.10 = (f32[8,3,18,1]{3,2,0,1:T(8,128)}, f32[8,3,18,1]{3,2,0,1:T(8,128)}, u32[]{:S(2)}, u32[]{:S(2)}) collective-permute-start(f32[8,3,18,1]{3,2,0,1:T(8,128)} %get-tuple-element.48), channel_id=1, source_target_pairs={{0,1},{1,2},{2,3},{3,4},{4,5},{5,6},{6,7},{8,9},{9,10},{10,11},{11... | collective-permute-start | bytes 5192 | tf_op jit(solution)/shard_map/ppermute | solution.py:14
  314.9 13.2 %all-to-all-start.5 = ((f32[3,32,40]{2,0,1:T(4,128)}), f32[3,32,40]{2,0,1:T(4,128)}, u32[]{:S(2)}, u32[]{:S(2)}) async-start(f32[3,32,40]{2,0,1:T(4,128)} %multiply_bitcast_fusion.3), calls=%async_computation.5 | async-start | bytes 131072 | tf_op jit(solution)/shard_map/all_to_all | solution.py:100
  400.4 32.3 %collective-permute-start.13 = (f32[8,3,1,128]{3,2,0,1:T(1,128)}, f32[8,3,1,128]{3,2,0,1:T(1,128)}, u32[]{:S(2)}, u32[]{:S(2)}) collective-permute-start(f32[8,3,1,128]{3,2,0,1:T(1,128)} %get-tuple-element.81), channel_id=1, source_target_pairs={{8,0},{16,8},{24,16},{9,1},{17,9},{25,17},{10,2},{18,10},{26,18},{... | collective-permute-start | bytes 36872 | tf_op jit(solution)/shard_map/ppermute | solution.py:17
  401.7 31.0 %collective-permute-start.12 = (f32[8,3,1,128]{3,2,0,1:T(1,128)}, f32[8,3,1,128]{3,2,0,1:T(1,128)}, u32[]{:S(2)}, u32[]{:S(2)}) collective-permute-start(f32[8,3,1,128]{3,2,0,1:T(1,128)} %get-tuple-element.80), channel_id=1, source_target_pairs={{0,8},{8,16},{16,24},{1,9},{9,17},{17,25},{2,10},{10,18},{18,26},{... | collective-permute-start | bytes 36872 | tf_op jit(solution)/shard_map/ppermute | solution.py:14
  428.8 11.1 %all-to-all-start.6 = ((f32[3,32,40]{2,0,1:T(4,128)}), f32[3,32,40]{2,0,1:T(4,128)}, u32[]{:S(2)}, u32[]{:S(2)}) async-start(f32[3,32,40]{2,0,1:T(4,128)} %bitcast.709), calls=%async_computation.6 | async-start | bytes 131072 | tf_op jit(solution)/shard_map/all_to_all | solution.py:96
  434.6 63.8 %collective-permute-start.15 = (f32[8,3,18,1]{3,2,0,1:T(8,128)}, f32[8,3,18,1]{3,2,0,1:T(8,128)}, u32[]{:S(2)}, u32[]{:S(2)}) collective-permute-start(f32[8,3,18,1]{3,2,0,1:T(8,128)} %get-tuple-element.47), channel_id=1, source_target_pairs={{1,0},{2,1},{3,2},{4,3},{5,4},{6,5},{7,6},{9,8},{10,9},{11,10},{12... | collective-permute-start | bytes 5192 | tf_op jit(solution)/shard_map/ppermute | solution.py:17
  435.9 62.6 %collective-permute-start.14 = (f32[8,3,18,1]{3,2,0,1:T(8,128)}, f32[8,3,18,1]{3,2,0,1:T(8,128)}, u32[]{:S(2)}, u32[]{:S(2)}) collective-permute-start(f32[8,3,18,1]{3,2,0,1:T(8,128)} %get-tuple-element.46), channel_id=1, source_target_pairs={{0,1},{1,2},{2,3},{3,4},{4,5},{5,6},{6,7},{8,9},{9,10},{10,11},{11... | collective-permute-start | bytes 5192 | tf_op jit(solution)/shard_map/ppermute | solution.py:14
  464.3 13.3 %all-to-all-start.7 = ((f32[3,32,40]{2,0,1:T(4,128)}), f32[3,32,40]{2,0,1:T(4,128)}, u32[]{:S(2)}, u32[]{:S(2)}) async-start(f32[3,32,40]{2,0,1:T(4,128)} %multiply_bitcast_fusion.2), calls=%async_computation.7 | async-start | bytes 131072 | tf_op jit(solution)/shard_map/all_to_all | solution.py:100
  544.3 26.5 %collective-permute-start.17 = (f32[8,3,1,128]{3,2,0,1:T(1,128)S(1)}, f32[8,3,1,128]{3,2,0,1:T(1,128)S(1)}, u32[]{:S(2)}, u32[]{:S(2)}) collective-permute-start(f32[8,3,1,128]{3,2,0,1:T(1,128)S(1)} %get-tuple-element.70), channel_id=1, source_target_pairs={{8,0},{16,8},{24,16},{9,1},{17,9},{25,17},{10,2},{18,10},{26,18},{... | collective-permute-start | bytes 36872 | tf_op jit(solution)/shard_map/ppermute | solution.py:17
  545.6 25.2 %collective-permute-start.16 = (f32[8,3,1,128]{3,2,0,1:T(1,128)S(1)}, f32[8,3,1,128]{3,2,0,1:T(1,128)S(1)}, u32[]{:S(2)}, u32[]{:S(2)}) collective-permute-start(f32[8,3,1,128]{3,2,0,1:T(1,128)S(1)} %get-tuple-element.69), channel_id=1, source_target_pairs={{0,8},{8,16},{16,24},{1,9},{9,17},{17,25},{2,10},{10,18},{18,26},{... | collective-permute-start | bytes 36872 | tf_op jit(solution)/shard_map/ppermute | solution.py:14
  551.1 27.0 %copy-start.25 = (f32[32,40,3]{1,2,0:T(4,128)S(1)}, f32[32,40,3]{1,2,0:T(4,128)}, u32[]{:S(2)}) copy-start(f32[32,40,3]{1,2,0:T(4,128)} %copy-done.24) | copy-start | bytes 46084
  551.2 35.6 %copy-start.23 = (s32[2048]{0:T(1024)S(1)}, s32[2048]{0:T(1024)}, u32[]{:S(2)}) copy-start(s32[2048]{0:T(1024)} %copy-done.22) | copy-start | bytes 24580
  566.4 11.8 %all-to-all-start.8 = ((f32[3,32,40]{2,0,1:T(4,128)}), f32[3,32,40]{2,0,1:T(4,128)S(1)}, u32[]{:S(2)}, u32[]{:S(2)}) async-start(f32[3,32,40]{2,0,1:T(4,128)} %bitcast.150), calls=%async_computation.8 | async-start | bytes 131072 | tf_op jit(solution)/shard_map/all_to_all | solution.py:96
  570.8 23.1 %copy-start.62 = (f32[8,3,1,128]{3,2,0,1:T(1,128)}, f32[8,3,1,128]{3,2,0,1:T(1,128)S(1)}, u32[]{:S(2)}) copy-start(f32[8,3,1,128]{3,2,0,1:T(1,128)S(1)} %collective-permute-done.17) | copy-start | bytes 36868
  570.8 23.1 %copy-start.64 = (f32[8,3,1,128]{3,2,0,1:T(1,128)}, f32[8,3,1,128]{3,2,0,1:T(1,128)S(1)}, u32[]{:S(2)}) copy-start(f32[8,3,1,128]{3,2,0,1:T(1,128)S(1)} %collective-permute-done.16) | copy-start | bytes 36868
  571.8 54.6 %collective-permute-start.19 = (f32[8,3,18,1]{3,2,0,1:T(8,128)}, f32[8,3,18,1]{3,2,0,1:T(8,128)}, u32[]{:S(2)}, u32[]{:S(2)}) collective-permute-start(f32[8,3,18,1]{3,2,0,1:T(8,128)} %get-tuple-element.45), channel_id=1, source_target_pairs={{1,0},{2,1},{3,2},{4,3},{5,4},{6,5},{7,6},{9,8},{10,9},{11,10},{12... | collective-permute-start | bytes 5192 | tf_op jit(solution)/shard_map/ppermute | solution.py:17
  573.1 53.3 %collective-permute-start.18 = (f32[8,3,18,1]{3,2,0,1:T(8,128)}, f32[8,3,18,1]{3,2,0,1:T(8,128)}, u32[]{:S(2)}, u32[]{:S(2)}) collective-permute-start(f32[8,3,18,1]{3,2,0,1:T(8,128)} %get-tuple-element.44), channel_id=1, source_target_pairs={{0,1},{1,2},{2,3},{3,4},{4,5},{5,6},{6,7},{8,9},{9,10},{10,11},{11... | collective-permute-start | bytes 5192 | tf_op jit(solution)/shard_map/ppermute | solution.py:14
  594.6 12.2 %all-to-all-start.9 = ((f32[3,32,40]{2,0,1:T(4,128)}), f32[3,32,40]{2,0,1:T(4,128)S(1)}, u32[]{:S(2)}, u32[]{:S(2)}) async-start(f32[3,32,40]{2,0,1:T(4,128)} %multiply_bitcast_fusion.1), calls=%async_computation.9 | async-start | bytes 131072 | tf_op jit(solution)/shard_map/all_to_all | solution.py:100
  608.1 60.6 %copy-start.27 = (f32[8,3,16,128]{3,2,0,1:T(8,128)S(1)}, f32[8,3,16,128]{3,2,0,1:T(8,128)}, u32[]{:S(2)}) copy-start(f32[8,3,16,128]{3,2,0,1:T(8,128)} %copy-done.26) | copy-start | bytes 589828
  608.1 60.6 %copy-start.29 = (f32[8,3,16,128]{3,2,0,1:T(8,128)S(1)}, f32[8,3,16,128]{3,2,0,1:T(8,128)}, u32[]{:S(2)}) copy-start(f32[8,3,16,128]{3,2,0,1:T(8,128)} %copy-done.28) | copy-start | bytes 589828
  608.1 60.6 %copy-start.31 = (f32[8,3,16,128]{3,2,0,1:T(8,128)S(1)}, f32[8,3,16,128]{3,2,0,1:T(8,128)}, u32[]{:S(2)}) copy-start(f32[8,3,16,128]{3,2,0,1:T(8,128)} %copy-done.30) | copy-start | bytes 589828
  608.1 60.6 %copy-start.33 = (f32[8,3,16,128]{3,2,0,1:T(8,128)S(1)}, f32[8,3,16,128]{3,2,0,1:T(8,128)}, u32[]{:S(2)}) copy-start(f32[8,3,16,128]{3,2,0,1:T(8,128)} %copy-done.32) | copy-start | bytes 589828
  608.1 60.6 %copy-start.37 = (f32[8,3,16,128]{3,2,1,0:T(8,128)S(1)}, f32[8,3,16,128]{3,2,1,0:T(8,128)}, u32[]{:S(2)}) copy-start(f32[8,3,16,128]{3,2,1,0:T(8,128)} %param.12) | copy-start | bytes 589828
  621.1 47.7 %copy-start.6 = (bf16[8,3,1,16,128]{4,3,2,1,0:T(8,128)(2,1)S(1)}, bf16[8,3,1,16,128]{4,3,2,1,0:T(8,128)(2,1)}, u32[]{:S(2)}) copy-start(bf16[8,3,1,16,128]{4,3,2,1,0:T(8,128)(2,1)} %copy-done.5) | copy-start | bytes 294916
  621.1 47.7 %copy-start.8 = (bf16[8,3,1,16,128]{4,3,2,1,0:T(8,128)(2,1)S(1)}, bf16[8,3,1,16,128]{4,3,2,1,0:T(8,128)(2,1)}, u32[]{:S(2)}) copy-start(bf16[8,3,1,16,128]{4,3,2,1,0:T(8,128)(2,1)} %copy-done.7) | copy-start | bytes 294916
  621.1 47.8 %copy-start.10 = (bf16[8,3,1,16,128]{4,3,2,1,0:T(8,128)(2,1)S(1)}, bf16[8,3,1,16,128]{4,3,2,1,0:T(8,128)(2,1)}, u32[]{:S(2)}) copy-start(bf16[8,3,1,16,128]{4,3,2,1,0:T(8,128)(2,1)} %copy-done.9) | copy-start | bytes 294916
  669.0 25.7 %collective-permute-start.21 = (f32[8,3,1,128]{3,2,0,1:T(1,128)S(1)}, f32[8,3,1,128]{3,2,0,1:T(1,128)S(1)}, u32[]{:S(2)}, u32[]{:S(2)}) collective-permute-start(f32[8,3,1,128]{3,2,0,1:T(1,128)S(1)} %get-tuple-element.63), channel_id=1, source_target_pairs={{8,0},{16,8},{24,16},{9,1},{17,9},{25,17},{10,2},{18,10},{26,18},{... | collective-permute-start | bytes 36872 | tf_op jit(solution)/shard_map/ppermute | solution.py:17
  670.3 24.4 %collective-permute-start.20 = (f32[8,3,1,128]{3,2,0,1:T(1,128)S(1)}, f32[8,3,1,128]{3,2,0,1:T(1,128)S(1)}, u32[]{:S(2)}, u32[]{:S(2)}) collective-permute-start(f32[8,3,1,128]{3,2,0,1:T(1,128)S(1)} %get-tuple-element.62), channel_id=1, source_target_pairs={{0,8},{8,16},{16,24},{1,9},{9,17},{17,25},{2,10},{10,18},{18,26},{... | collective-permute-start | bytes 36872 | tf_op jit(solution)/shard_map/ppermute | solution.py:14
  690.2 11.8 %all-to-all-start.10 = ((f32[3,32,40]{2,0,1:T(4,128)}), f32[3,32,40]{2,0,1:T(4,128)S(1)}, u32[]{:S(2)}, u32[]{:S(2)}) async-start(f32[3,32,40]{2,0,1:T(4,128)} %bitcast.167), calls=%async_computation.10 | async-start | bytes 131072 | tf_op jit(solution)/shard_map/all_to_all | solution.py:96
  695.6 53.4 %collective-permute-start.23 = (f32[8,3,18,1]{3,2,0,1:T(8,128)}, f32[8,3,18,1]{3,2,0,1:T(8,128)}, u32[]{:S(2)}, u32[]{:S(2)}) collective-permute-start(f32[8,3,18,1]{3,2,0,1:T(8,128)} %get-tuple-element.43), channel_id=1, source_target_pairs={{1,0},{2,1},{3,2},{4,3},{5,4},{6,5},{7,6},{9,8},{10,9},{11,10},{12... | collective-permute-start | bytes 5192 | tf_op jit(solution)/shard_map/ppermute | solution.py:17
  696.9 52.1 %collective-permute-start.22 = (f32[8,3,18,1]{3,2,0,1:T(8,128)}, f32[8,3,18,1]{3,2,0,1:T(8,128)}, u32[]{:S(2)}, u32[]{:S(2)}) collective-permute-start(f32[8,3,18,1]{3,2,0,1:T(8,128)} %get-tuple-element.42), channel_id=1, source_target_pairs={{0,1},{1,2},{2,3},{3,4},{4,5},{5,6},{6,7},{8,9},{9,10},{10,11},{11... | collective-permute-start | bytes 5192 | tf_op jit(solution)/shard_map/ppermute | solution.py:14
  718.5 12.2 %all-to-all-start.11 = ((f32[3,32,40]{2,0,1:T(4,128)}), f32[3,32,40]{2,0,1:T(4,128)S(1)}, u32[]{:S(2)}, u32[]{:S(2)}) async-start(f32[3,32,40]{2,0,1:T(4,128)} %multiply_bitcast_fusion), calls=%async_computation.11 | async-start | bytes 131072 | tf_op jit(solution)/shard_map/all_to_all | solution.py:100
  (45 other events, 455.9 us)
where the time goes:
time: 764 us; the launch traced here: 752 us
  local copies, waits for them, and re-layouts  242 us (32%)
  other arithmetic  169 us (22%)
  blocking collectives  154 us (20%)
  starting transfers between devices  129 us (17%)
  waiting for transfers between devices  38.7 us (5%)
  between operations  13.2 us (2%)
    unnamed x9, other arithmetic  77.9 us
    psum x2, blocking collectives, per_device(): lax.psum((jnp.sum(response * halfway), jnp.sum(response * response), jnp....  77.2 us
    gather x12, local copies, waits for them, and re-layouts, well_term(): values = flattened[layer_idx, :, column_idx]  75.5 us
    gather x12, local copies, waits for them, and re-layouts, solve_wells(): return padded[targets]  55.7 us
    ppermute x12, starting transfers between devices, padded_2(): lax.ppermute(lax.slice_in_dim(block, block.shape[dim] - width, None, axis...  52.9 us
    unnamed x176, local copies, waits for them, and re-layouts  45.4 us
    scatter-add x6, other arithmetic, solve_wells(): totals = jnp.zeros((per_owner + 1,), jnp.float32).at[targets].add(rate)  44.8 us
    psum x1, blocking collectives, per_device(): inner_now = lax.psum(jnp.sum(shadow * residual), ('gx', 'gy'))  38.8 us
  transfers between devices with their start and end apart: 36, of which 11 were waited for; matrix products, arithmetic and copies ran while one was open for 49% of the time, Pallas kernels for 0%

commit v1 on v0

--- a/solution.py
+++ b/solution.py
@@ -2,6 +2,7 @@
 import jax.numpy as jnp
 from jax import lax
 from jax.sharding import PartitionSpec as P
+from jax.lax import all_to_all, axis_size
 
 ITERS = 2
 
@@ -97,8 +98,12 @@
         coeff_in = pad_in[:, targets]
         rate = coeff_in[0] * arrived[0] + coeff_in[1] * arrived[1] + coeff_in[2] * arrived[2]
         back = solve_wells(rate)
-        terms = lax.all_to_all(
-            pad_out[:, targets] * back[None], ("gx", "gy"), split_axis=1, concat_axis=1, tiled=True
+        my_tile = pad_out[:, targets] * back[None]
+        terms = jnp.concatenate(
+            all_to_all(
+                jnp.stack(jnp.split(my_tile, axis_size(("gx", "gy")), 1)), ("gx", "gy"), 0, 0
+            ),
+            axis=1,
         )
         scattered = (
             jnp.zeros((layers, comps, tile_area), jnp.float32)

time: 764 us -> 787 us (1.030)
  local copies, waits for them, and re-layouts: 242 us -> 268 us
    another operation x0 -> x24, local copies, waits for them, and re-layouts: none -> 26.8 us  [well_term(): jnp.stack(jnp.split(my_tile, axis_size(('gx', 'gy')), 1))]
  transfers between devices with their start and end apart: 36 -> 36, of which waited for: 11 -> 11; matrix products, arithmetic and copies ran while one was open for 49% -> 50% of each run, Pallas kernels for 0% -> 0%
where the time goes in v1:
time: 787 us; the launch traced here: 774 us
  local copies, waits for them, and re-layouts  268 us (34%)
  other arithmetic  165 us (21%)
  blocking collectives  154 us (20%)
  starting transfers between devices  129 us (16%)
  waiting for transfers between devices  38.9 us (5%)
  between operations  13.1 us (2%)
    unnamed x9, other arithmetic  78.1 us
    psum x2, blocking collectives, per_device(): lax.psum((jnp.sum(response * halfway), jnp.sum(response * response), jnp....  77.2 us
    gather x12, local copies, waits for them, and re-layouts, well_term(): values = flattened[layer_idx, :, column_idx]  75.6 us
    gather x12, local copies, waits for them, and re-layouts, solve_wells(): return padded[targets]  55.7 us
    ppermute x12, starting transfers between devices, padded_2(): lax.ppermute(lax.slice_in_dim(block, block.shape[dim] - width, None, axis...  52.8 us
    unnamed x176, local copies, waits for them, and re-layouts  45.4 us
    scatter-add x6, other arithmetic, solve_wells(): totals = jnp.zeros((per_owner + 1,), jnp.float32).at[targets].add(rate)  44.8 us
    psum x1, blocking collectives, per_device(): inner_now = lax.psum(jnp.sum(shadow * residual), ('gx', 'gy'))  38.8 us
  transfers between devices with their start and end apart: 36, of which 11 were waited for; matrix products, arithmetic and copies ran while one was open for 50% of the time, Pallas kernels for 0%

profile of v1, /device:TPU:0, one launch (start us, length us, event | category | flops | bytes accessed | tf_op | source)
XLA Modules:
  0.0 774.3 jit_solution(2962961475071824413)
XLA Ops:
  1.6 5.7 copy.640
  7.4 9.6 %gather_fusion.2 = f32[1280,3]{1,0:T(8,128)S(1)} fusion(f32[8,3,2048]{1,2,0:T(8,128)} %bitcast.1005, s32[1280]{0:T(1024)S(1)} %reshape.544), kind=kCustom, calls=%fused_computation.2 | custom fusion | bytes 40960 | tf_op jit(solution)/shard_map/gather | solution.py:95
  17.8 7.3 all-to-all-start
  26.7 4.5 collective-permute-start
  50.0 7.3 scatter_custom_fusion
  58.3 7.1 gather_fusion.3
  66.4 6.4 all-to-all-start.1
  73.5 6.7 all-to-all-done.1
  81.3 13.2 %scatter_custom_fusion.6 = f32[3,16384]{0,1:T(8,128)} fusion(s32[1280]{0:T(1024)S(1)} %reshape.676, f32[1280,3]{1,0:T(8,128)} %bitcast.1056, f32[]{:T(128)} %constant.32.clone.1), kind=kCustom, calls=%fused_computation.36 | custom fusion | flops 3840 | bytes 197120
  94.4 5.9 copy.646
  106.7 5.1 collective-permute-start.4
  113.3 5.6 copy.667
  118.9 12.7 %gather_fusion.4 = f32[1280,3]{1,0:T(8,128)} fusion(f32[8,3,2048]{1,2,0:T(8,128)} %copy.667, s32[1280]{0:T(1024)S(1)} %reshape.544), kind=kCustom, calls=%fused_computation.4 | custom fusion | bytes 40960 | tf_op jit(solution)/shard_map/gather | solution.py:95
  147.4 7.5 scatter_custom_fusion.1
  155.9 10.0 %gather_fusion.5 = f32[1280]{0:T(1024)} fusion(f32[1025]{0:T(1024)S(1)} %pad_maximum_fusion.58, s32[2048]{0:T(1024)} %copy-done.22), kind=kCustom, calls=%fused_computation.5 | custom fusion | bytes 15360 | tf_op jit(solution)/shard_map/gather | solution.py:91
  169.4 5.3 stack.659
  176.2 5.8 all-to-all-start.3
  183.7 5.5 all-to-all-done.3
  191.2 13.0 %scatter_custom_fusion.7 = f32[3,16384]{0,1:T(8,128)} fusion(s32[1280]{0:T(1024)} %copy-done.70, f32[1280,3]{1,0:T(8,128)} %bitcast.1057, f32[]{:T(128)} %constant.32.clone.1), kind=kCustom, calls=%fused_computation.34 | custom fusion | flops 3840 | bytes 197120
  204.2 5.9 copy.673
  213.6 38.8 %all-reduce.16 = (f32[]{:T(128)}, f32[]{:T(128)}) all-reduce(f32[]{:T(128)} %get-tuple-element.22, f32[]{:T(128)} %get-tuple-element.21), channel_id=1, replica_groups=mesh['gx'=4,'gy'=8] {'gx','gy'}, use_global_device_ids=true, to_apply=%region_3.4 | all-reduce | flops 2 | bytes 16 | tf_op jit(solution)/shard_map/psum | solution.py:123
  259.6 5.4 collective-permute-start.8
  266.4 5.6 copy.688
  272.0 12.7 %gather_fusion.6 = f32[1280,3]{1,0:T(8,128)} fusion(f32[8,3,2048]{1,2,0:T(8,128)} %copy.688, s32[1280]{0:T(1024)S(1)} %reshape.544), kind=kCustom, calls=%fused_computation.6 | custom fusion | bytes 40960 | tf_op jit(solution)/shard_map/gather | solution.py:95
  301.0 7.5 scatter_custom_fusion.2
  309.4 10.0 %gather_fusion.7 = f32[1280]{0:T(1024)} fusion(f32[1025]{0:T(1024)S(1)} %pad_maximum_fusion.57, s32[2048]{0:T(1024)} %copy-done.22), kind=kCustom, calls=%fused_computation.7 | custom fusion | bytes 15360 | tf_op jit(solution)/shard_map/gather | solution.py:91
  322.9 5.3 stack.692
  329.7 5.9 all-to-all-start.5
  338.7 4.3 all-to-all-done.5
  344.9 13.0 %scatter_custom_fusion.8 = f32[3,16384]{0,1:T(8,128)} fusion(s32[1280]{0:T(1024)} %copy-done.70, f32[1280,3]{1,0:T(8,128)} %bitcast.1058, f32[]{:T(128)} %constant.32.clone.1), kind=kCustom, calls=%fused_computation.32 | custom fusion | flops 3840 | bytes 197120
  357.9 5.9 copy.694
  367.3 38.5 %all-reduce.15 = (f32[]{:T(128)}, f32[]{:T(128)}, f32[]{:T(128)}) all-reduce(f32[]{:T(128)} %get-tuple-element.20, f32[]{:T(128)} %get-tuple-element.19, f32[]{:T(128)} %get-tuple-element.18), channel_id=1, replica_groups=mesh['gx'=4,'gy'=8] {'gx','gy'}, use_global_device_ids=true, to_apply=%region_11.12 | all-reduce | flops 3 | bytes 24 | tf_op jit(solution)/shard_map/psum | solution.py:133
  416.4 5.4 collective-permute-start.12
  423.2 5.6 copy.708
  428.8 12.7 %gather_fusion.8 = f32[1280,3]{1,0:T(8,128)} fusion(f32[8,3,2048]{1,2,0:T(8,128)} %copy.708, s32[1280]{0:T(1024)S(1)} %reshape.544), kind=kCustom, calls=%fused_computation.8 | custom fusion | bytes 40960 | tf_op jit(solution)/shard_map/gather | solution.py:95
  458.0 7.5 scatter_custom_fusion.3
  466.4 10.0 %gather_fusion.9 = f32[1280]{0:T(1024)} fusion(f32[1025]{0:T(1024)S(1)} %pad_maximum_fusion.56, s32[2048]{0:T(1024)} %copy-done.22), kind=kCustom, calls=%fused_computation.9 | custom fusion | bytes 15360 | tf_op jit(solution)/shard_map/gather | solution.py:91
  479.9 5.3 stack.725
  486.7 5.8 all-to-all-start.7
  494.3 5.5 all-to-all-done.7
  501.8 13.0 %scatter_custom_fusion.9 = f32[3,16384]{0,1:T(8,128)} fusion(s32[1280]{0:T(1024)} %copy-done.70, f32[1280,3]{1,0:T(8,128)} %bitcast.1059, f32[]{:T(128)} %constant.32.clone.1), kind=kCustom, calls=%fused_computation.30 | custom fusion | flops 3840 | bytes 197120
  514.7 5.9 copy.714
  524.1 38.5 %psum.61 = f32[]{:T(128)} all-reduce(f32[]{:T(128)} %get-tuple-element.30), channel_id=1, replica_groups=mesh['gx'=4,'gy'=8] {'gx','gy'}, use_global_device_ids=true, to_apply=%region_19.20 | all-reduce | flops 1 | bytes 8 | tf_op jit(solution)/shard_map/psum | solution.py:128
  567.9 4.8 collective-permute-start.16
  573.5 4.7 copy.728
  578.1 9.6 %gather_fusion.10 = f32[1280,3]{1,0:T(8,128)S(1)} fusion(f32[8,3,2048]{1,2,0:T(8,128)} %copy.728, s32[1280]{0:T(1024)S(1)} %reshape.544), kind=kCustom, calls=%fused_computation.10 | custom fusion | bytes 40960 | tf_op jit(solution)/shard_map/gather | solution.py:95
  588.6 4.4 all-to-all-start.8
  600.5 7.5 scatter_custom_fusion.4
  609.0 7.1 gather_fusion.11
  617.1 4.8 all-to-all-start.9
  622.6 6.6 all-to-all-done.9
  630.5 13.0 %scatter_custom_fusion.10 = f32[3,16384]{0,1:T(8,128)} fusion(s32[1280]{0:T(1024)} %copy-done.70, f32[1280,3]{1,0:T(8,128)} %bitcast.1060, f32[]{:T(128)} %constant.32.clone.1), kind=kCustom, calls=%fused_computation.28 | custom fusion | flops 3840 | bytes 197120
  643.5 5.3 copy.734
  651.2 38.6 %all-reduce.14 = (f32[]{:T(128)}, f32[]{:T(128)}) all-reduce(f32[]{:T(128)} %get-tuple-element.17, f32[]{:T(128)} %get-tuple-element.16), channel_id=1, replica_groups=mesh['gx'=4,'gy'=8] {'gx','gy'}, use_global_device_ids=true, to_apply=%region_23.24 | all-reduce | flops 2 | bytes 16 | tf_op jit(solution)/shard_map/psum | solution.py:133
  692.8 4.8 collective-permute-start.20
  697.6 4.7 copy.735
  702.3 9.6 %gather_fusion.12 = f32[1280,3]{1,0:T(8,128)S(1)} fusion(f32[8,3,2048]{1,2,0:T(8,128)} %bitcast.1006, s32[1280]{0:T(1024)S(1)} %reshape.544), kind=kCustom, calls=%fused_computation.12 | custom fusion | bytes 40960 | tf_op jit(solution)/shard_map/gather | solution.py:95
  712.8 4.4 all-to-all-start.10
  724.7 7.5 scatter_custom_fusion.5
  733.2 7.1 gather_fusion.13
  741.2 4.8 all-to-all-start.11
  746.7 6.6 all-to-all-done.11
  753.6 12.9 %scatter_custom_fusion.11 = f32[3,16384]{0,1:T(8,128)} fusion(s32[1280]{0:T(1024)} %copy-done.70, f32[1280,3]{1,0:T(8,128)S(1)} %bitcast.1055, f32[]{:T(128)} %constant.32.clone.1), kind=kCustom, calls=%fused_computation.26 | custom fusion | flops 3840 | bytes 197120
  766.5 5.2 copy.741
  (409 shorter events, 169.2 us)
Async XLA Ops:
  0.6 56.7 %copy-start = (f32[8,128,128]{2,1,0:T(8,128)S(1)}, f32[8,128,128]{2,1,0:T(8,128)}, u32[]{:S(2)}) copy-start(f32[8,128,128]{2,1,0:T(8,128)} %param.21) | copy-start | bytes 1572868
  0.6 24.5 %copy-start.36 = (f32[8,3,16,128]{3,2,1,0:T(8,128)S(1)}, f32[8,3,16,128]{3,2,1,0:T(8,128)}, u32[]{:S(2)}) copy-start(f32[8,3,16,128]{3,2,1,0:T(8,128)} %param.12) | copy-start | bytes 589828
  0.7 24.5 %copy-start.57 = (bf16[8,3,3,16,128]{4,3,2,1,0:T(8,128)(2,1)S(1)}, bf16[8,3,3,16,128]{4,3,2,1,0:T(8,128)(2,1)}, u32[]{:S(2)}) copy-start(bf16[8,3,3,16,128]{4,3,2,1,0:T(8,128)(2,1)} %param.14) | copy-start | bytes 884740
  1.5 30.6 %copy-start.39 = (bf16[4,6,6,16,128]{4,3,2,1,0:T(8,128)(2,1)S(1)}, bf16[4,6,6,16,128]{4,3,2,1,0:T(8,128)(2,1)}, u32[]{:S(2)}) copy-start(bf16[4,6,6,16,128]{4,3,2,1,0:T(8,128)(2,1)} %param.16) | copy-start | bytes 1769476
  1.5 30.7 %copy-start.71 = (s32[2]{0:T(128)S(1)}, s32[2]{0:T(128)}, u32[]{:S(2)}) copy-start(s32[2]{0:T(128)} %constant.76) | copy-start | bytes 28
  1.5 30.8 %copy-start.72 = (s32[2]{0:T(128)S(1)}, s32[2]{0:T(128)}, u32[]{:S(2)}) copy-start(s32[2]{0:T(128)} %constant.73) | copy-start | bytes 28
  1.5 30.9 %copy-start.69 = (s32[1,32,40]{2,1,0:T(8,128)S(1)}, s32[1,32,40]{2,1,0:T(8,128)}, u32[]{:S(2)}) copy-start(s32[1,32,40]{2,1,0:T(8,128)} %param.18) | copy-start | bytes 15364
  1.5 30.9 %copy-start.59 = (bf16[6,8,16,128]{3,2,1,0:T(8,128)(2,1)S(1)}, bf16[6,8,16,128]{3,2,1,0:T(8,128)(2,1)}, u32[]{:S(2)}) copy-start(bf16[6,8,16,128]{3,2,1,0:T(8,128)(2,1)} %param.15) | copy-start | bytes 589828
  7.3 26.1 %copy-start.58 = (bf16[8,3,3,16,128]{4,3,2,1,0:T(8,128)(2,1)S(1)}, bf16[8,3,3,16,128]{4,3,2,1,0:T(8,128)(2,1)}, u32[]{:S(2)}) copy-start(bf16[8,3,3,16,128]{4,3,2,1,0:T(8,128)(2,1)} %param.13) | copy-start | bytes 884740
  7.3 26.8 %copy-start.67 = (f32[3,1024]{1,0:T(4,128)S(1)}, f32[3,1024]{1,0:T(4,128)}, u32[]{:S(2)}) copy-start(f32[3,1024]{1,0:T(4,128)} %param.20) | copy-start | bytes 36868
  7.3 31.6 %copy-start.68 = (f32[3,1024]{1,0:T(4,128)S(1)}, f32[3,1024]{1,0:T(4,128)}, u32[]{:S(2)}) copy-start(f32[3,1024]{1,0:T(4,128)} %param.19) | copy-start | bytes 36868
  17.8 31.9 %all-to-all-start = ((f32[3,32,40]{2,0,1:T(4,128)}), f32[3,32,40]{2,0,1:T(4,128)S(1)}, u32[]{:S(2)}, u32[]{:S(2)}) async-start(f32[3,32,40]{2,0,1:T(4,128)} %bitcast.22), calls=%async_computation | async-start | bytes 131072 | tf_op jit(solution)/shard_map/all_to_all | solution.py:97
  25.4 32.9 %copy-start.11 = (f32[8,3,16,128]{3,2,0,1:T(8,128)}, f32[8,3,16,128]{3,2,0,1:T(8,128)S(1)}, u32[]{:S(2)}) copy-start(f32[8,3,16,128]{3,2,0,1:T(8,128)S(1)} %fusion.39) | copy-start | bytes 589828
  25.4 18.3 %collective-permute-start.1 = (f32[8,3,1,128]{3,2,0,1:T(1,128)S(1)}, f32[8,3,1,128]{3,2,0,1:T(1,128)S(1)}, u32[]{:S(2)}, u32[]{:S(2)}) collective-permute-start(f32[8,3,1,128]{3,2,0,1:T(1,128)S(1)} %get-tuple-element.126), channel_id=1, source_target_pairs={{8,0},{16,8},{24,16},{9,1},{17,9},{25,17},{10,2},{18,10},{26,18},{... | collective-permute-start | bytes 36872 | tf_op jit(solution)/shard_map/ppermute | solution.py:18
  26.7 17.0 %collective-permute-start = (f32[8,3,1,128]{3,2,0,1:T(1,128)S(1)}, f32[8,3,1,128]{3,2,0,1:T(1,128)S(1)}, u32[]{:S(2)}, u32[]{:S(2)}) collective-permute-start(f32[8,3,1,128]{3,2,0,1:T(1,128)S(1)} %get-tuple-element.125), channel_id=1, source_target_pairs={{0,8},{8,16},{16,24},{1,9},{9,17},{17,25},{2,10},{10,18},{18,26},{... | collective-permute-start | bytes 36872 | tf_op jit(solution)/shard_map/ppermute | solution.py:15
  32.5 32.9 %copy-start.66 = (s32[1280]{0:T(1024)}, s32[1280]{0:T(1024)S(1)}, u32[]{:S(2)}) copy-start(s32[1280]{0:T(1024)S(1)} %reshape.530) | copy-start | bytes 15364
  34.1 31.3 %copy-start.22 = (s32[2048]{0:T(1024)}, s32[2048]{0:T(1024)S(1)}, u32[]{:S(2)}) copy-start(s32[2048]{0:T(1024)S(1)} %pad_clamp_fusion) | copy-start | bytes 24580
  38.9 26.6 %copy-start.20 = (f32[32,40,3]{1,0,2:T(8,128)}, f32[32,40,3]{1,0,2:T(8,128)S(1)}, u32[]{:S(2)}) copy-start(f32[32,40,3]{1,0,2:T(8,128)S(1)} %copy.642) | copy-start | bytes 46084
  44.7 55.6 %collective-permute-start.3 = (f32[8,3,18,1]{3,2,0,1:T(8,128)}, f32[8,3,18,1]{3,2,0,1:T(8,128)}, u32[]{:S(2)}, u32[]{:S(2)}) collective-permute-start(f32[8,3,18,1]{3,2,0,1:T(8,128)} %get-tuple-element.60), channel_id=1, source_target_pairs={{1,0},{2,1},{3,2},{4,3},{5,4},{6,5},{7,6},{9,8},{10,9},{11,10},{12... | collective-permute-start | bytes 5192 | tf_op jit(solution)/shard_map/ppermute | solution.py:18
  46.0 54.3 %collective-permute-start.2 = (f32[8,3,18,1]{3,2,0,1:T(8,128)}, f32[8,3,18,1]{3,2,0,1:T(8,128)}, u32[]{:S(2)}, u32[]{:S(2)}) collective-permute-start(f32[8,3,18,1]{3,2,0,1:T(8,128)} %get-tuple-element.59), channel_id=1, source_target_pairs={{0,1},{1,2},{2,3},{3,4},{4,5},{5,6},{6,7},{8,9},{9,10},{10,11},{11... | collective-permute-start | bytes 5192 | tf_op jit(solution)/shard_map/ppermute | solution.py:15
  66.4 13.8 %all-to-all-start.1 = ((f32[32,3,1,40]{3,2,1,0:T(1,128)}), f32[32,3,1,40]{3,2,1,0:T(1,128)S(1)}, u32[]{:S(2)}, u32[]{:S(2)}) async-start(f32[32,3,1,40]{3,2,1,0:T(1,128)} %copy.643), calls=%async_computation.1 | async-start | bytes 98304 | tf_op jit(solution)/shard_map/all_to_all | solution.py:103
  72.9 27.4 %copy-start.70 = (s32[1280]{0:T(1024)}, s32[1280]{0:T(1024)S(1)}, u32[]{:S(2)}) copy-start(s32[1280]{0:T(1024)S(1)} %reshape.676) | copy-start | bytes 15364
  105.4 31.5 %collective-permute-start.5 = (f32[8,3,1,128]{3,2,0,1:T(1,128)}, f32[8,3,1,128]{3,2,0,1:T(1,128)}, u32[]{:S(2)}, u32[]{:S(2)}) collective-permute-start(f32[8,3,1,128]{3,2,0,1:T(1,128)} %get-tuple-element.111), channel_id=1, source_target_pairs={{8,0},{16,8},{24,16},{9,1},{17,9},{25,17},{10,2},{18,10},{26,18},{... | collective-permute-start | bytes 36872 | tf_op jit(solution)/shard_map/ppermute | solution.py:18
  106.7 30.3 %collective-permute-start.4 = (f32[8,3,1,128]{3,2,0,1:T(1,128)}, f32[8,3,1,128]{3,2,0,1:T(1,128)}, u32[]{:S(2)}, u32[]{:S(2)}) collective-permute-start(f32[8,3,1,128]{3,2,0,1:T(1,128)} %get-tuple-element.110), channel_id=1, source_target_pairs={{0,8},{8,16},{16,24},{1,9},{9,17},{17,25},{2,10},{10,18},{18,26},{... | collective-permute-start | bytes 36872 | tf_op jit(solution)/shard_map/ppermute | solution.py:15
  133.6 10.6 %all-to-all-start.2 = ((f32[3,32,40]{2,0,1:T(4,128)}), f32[3,32,40]{2,0,1:T(4,128)}, u32[]{:S(2)}, u32[]{:S(2)}) async-start(f32[3,32,40]{2,0,1:T(4,128)} %bitcast.1127), calls=%async_computation.2 | async-start | bytes 131072 | tf_op jit(solution)/shard_map/all_to_all | solution.py:97
  138.8 71.2 %collective-permute-start.7 = (f32[8,3,18,1]{3,2,0,1:T(8,128)}, f32[8,3,18,1]{3,2,0,1:T(8,128)}, u32[]{:S(2)}, u32[]{:S(2)}) collective-permute-start(f32[8,3,18,1]{3,2,0,1:T(8,128)} %get-tuple-element.55), channel_id=1, source_target_pairs={{1,0},{2,1},{3,2},{4,3},{5,4},{6,5},{7,6},{9,8},{10,9},{11,10},{12... | collective-permute-start | bytes 5192 | tf_op jit(solution)/shard_map/ppermute | solution.py:18
  140.1 70.0 %collective-permute-start.6 = (f32[8,3,18,1]{3,2,0,1:T(8,128)}, f32[8,3,18,1]{3,2,0,1:T(8,128)}, u32[]{:S(2)}, u32[]{:S(2)}) collective-permute-start(f32[8,3,18,1]{3,2,0,1:T(8,128)} %get-tuple-element.54), channel_id=1, source_target_pairs={{0,1},{1,2},{2,3},{3,4},{4,5},{5,6},{6,7},{8,9},{9,10},{10,11},{11... | collective-permute-start | bytes 5192 | tf_op jit(solution)/shard_map/ppermute | solution.py:15
  176.2 13.1 %all-to-all-start.3 = ((f32[32,3,1,40]{3,2,1,0:T(1,128)}), f32[32,3,1,40]{3,2,1,0:T(1,128)}, u32[]{:S(2)}, u32[]{:S(2)}) async-start(f32[32,3,1,40]{3,2,1,0:T(1,128)} %copy.670), calls=%async_computation.3 | async-start | bytes 98304 | tf_op jit(solution)/shard_map/all_to_all | solution.py:103
  258.3 32.3 %collective-permute-start.9 = (f32[8,3,1,128]{3,2,0,1:T(1,128)}, f32[8,3,1,128]{3,2,0,1:T(1,128)}, u32[]{:S(2)}, u32[]{:S(2)}) collective-permute-start(f32[8,3,1,128]{3,2,0,1:T(1,128)} %get-tuple-element.98), channel_id=1, source_target_pairs={{8,0},{16,8},{24,16},{9,1},{17,9},{25,17},{10,2},{18,10},{26,18},{... | collective-permute-start | bytes 36872 | tf_op jit(solution)/shard_map/ppermute | solution.py:18
  259.6 31.0 %collective-permute-start.8 = (f32[8,3,1,128]{3,2,0,1:T(1,128)}, f32[8,3,1,128]{3,2,0,1:T(1,128)}, u32[]{:S(2)}, u32[]{:S(2)}) collective-permute-start(f32[8,3,1,128]{3,2,0,1:T(1,128)} %get-tuple-element.97), channel_id=1, source_target_pairs={{0,8},{8,16},{16,24},{1,9},{9,17},{17,25},{2,10},{10,18},{18,26},{... | collective-permute-start | bytes 36872 | tf_op jit(solution)/shard_map/ppermute | solution.py:15
  286.7 11.1 %all-to-all-start.4 = ((f32[3,32,40]{2,0,1:T(4,128)}), f32[3,32,40]{2,0,1:T(4,128)}, u32[]{:S(2)}, u32[]{:S(2)}) async-start(f32[3,32,40]{2,0,1:T(4,128)} %bitcast.1128), calls=%async_computation.4 | async-start | bytes 131072 | tf_op jit(solution)/shard_map/all_to_all | solution.py:97
  292.6 71.2 %collective-permute-start.11 = (f32[8,3,18,1]{3,2,0,1:T(8,128)}, f32[8,3,18,1]{3,2,0,1:T(8,128)}, u32[]{:S(2)}, u32[]{:S(2)}) collective-permute-start(f32[8,3,18,1]{3,2,0,1:T(8,128)} %get-tuple-element.53), channel_id=1, source_target_pairs={{1,0},{2,1},{3,2},{4,3},{5,4},{6,5},{7,6},{9,8},{10,9},{11,10},{12... | collective-permute-start | bytes 5192 | tf_op jit(solution)/shard_map/ppermute | solution.py:18
  293.8 69.9 %collective-permute-start.10 = (f32[8,3,18,1]{3,2,0,1:T(8,128)}, f32[8,3,18,1]{3,2,0,1:T(8,128)}, u32[]{:S(2)}, u32[]{:S(2)}) collective-permute-start(f32[8,3,18,1]{3,2,0,1:T(8,128)} %get-tuple-element.52), channel_id=1, source_target_pairs={{0,1},{1,2},{2,3},{3,4},{4,5},{5,6},{6,7},{8,9},{9,10},{10,11},{11... | collective-permute-start | bytes 5192 | tf_op jit(solution)/shard_map/ppermute | solution.py:15
  329.7 13.2 %all-to-all-start.5 = ((f32[32,3,1,40]{3,2,1,0:T(1,128)}), f32[32,3,1,40]{3,2,1,0:T(1,128)}, u32[]{:S(2)}, u32[]{:S(2)}) async-start(f32[32,3,1,40]{3,2,1,0:T(1,128)} %copy.691), calls=%async_computation.5 | async-start | bytes 98304 | tf_op jit(solution)/shard_map/all_to_all | solution.py:103
  415.1 32.3 %collective-permute-start.13 = (f32[8,3,1,128]{3,2,0,1:T(1,128)}, f32[8,3,1,128]{3,2,0,1:T(1,128)}, u32[]{:S(2)}, u32[]{:S(2)}) collective-permute-start(f32[8,3,1,128]{3,2,0,1:T(1,128)} %get-tuple-element.85), channel_id=1, source_target_pairs={{8,0},{16,8},{24,16},{9,1},{17,9},{25,17},{10,2},{18,10},{26,18},{... | collective-permute-start | bytes 36872 | tf_op jit(solution)/shard_map/ppermute | solution.py:18
  416.4 31.0 %collective-permute-start.12 = (f32[8,3,1,128]{3,2,0,1:T(1,128)}, f32[8,3,1,128]{3,2,0,1:T(1,128)}, u32[]{:S(2)}, u32[]{:S(2)}) collective-permute-start(f32[8,3,1,128]{3,2,0,1:T(1,128)} %get-tuple-element.84), channel_id=1, source_target_pairs={{0,8},{8,16},{16,24},{1,9},{9,17},{17,25},{2,10},{10,18},{18,26},{... | collective-permute-start | bytes 36872 | tf_op jit(solution)/shard_map/ppermute | solution.py:15
  443.5 11.3 %all-to-all-start.6 = ((f32[3,32,40]{2,0,1:T(4,128)}), f32[3,32,40]{2,0,1:T(4,128)}, u32[]{:S(2)}, u32[]{:S(2)}) async-start(f32[3,32,40]{2,0,1:T(4,128)} %bitcast.1129), calls=%async_computation.6 | async-start | bytes 131072 | tf_op jit(solution)/shard_map/all_to_all | solution.py:97
  449.3 71.3 %collective-permute-start.15 = (f32[8,3,18,1]{3,2,0,1:T(8,128)}, f32[8,3,18,1]{3,2,0,1:T(8,128)}, u32[]{:S(2)}, u32[]{:S(2)}) collective-permute-start(f32[8,3,18,1]{3,2,0,1:T(8,128)} %get-tuple-element.51), channel_id=1, source_target_pairs={{1,0},{2,1},{3,2},{4,3},{5,4},{6,5},{7,6},{9,8},{10,9},{11,10},{12... | collective-permute-start | bytes 5192 | tf_op jit(solution)/shard_map/ppermute | solution.py:18
  450.6 70.0 %collective-permute-start.14 = (f32[8,3,18,1]{3,2,0,1:T(8,128)}, f32[8,3,18,1]{3,2,0,1:T(8,128)}, u32[]{:S(2)}, u32[]{:S(2)}) collective-permute-start(f32[8,3,18,1]{3,2,0,1:T(8,128)} %get-tuple-element.50), channel_id=1, source_target_pairs={{0,1},{1,2},{2,3},{3,4},{4,5},{5,6},{6,7},{8,9},{9,10},{10,11},{11... | collective-permute-start | bytes 5192 | tf_op jit(solution)/shard_map/ppermute | solution.py:15
  486.7 13.1 %all-to-all-start.7 = ((f32[32,3,1,40]{3,2,1,0:T(1,128)}), f32[32,3,1,40]{3,2,1,0:T(1,128)}, u32[]{:S(2)}, u32[]{:S(2)}) async-start(f32[32,3,1,40]{3,2,1,0:T(1,128)} %copy.711), calls=%async_computation.7 | async-start | bytes 98304 | tf_op jit(solution)/shard_map/all_to_all | solution.py:103
  566.6 26.4 %collective-permute-start.17 = (f32[8,3,1,128]{3,2,0,1:T(1,128)S(1)}, f32[8,3,1,128]{3,2,0,1:T(1,128)S(1)}, u32[]{:S(2)}, u32[]{:S(2)}) collective-permute-start(f32[8,3,1,128]{3,2,0,1:T(1,128)S(1)} %get-tuple-element.74), channel_id=1, source_target_pairs={{8,0},{16,8},{24,16},{9,1},{17,9},{25,17},{10,2},{18,10},{26,18},{... | collective-permute-start | bytes 36872 | tf_op jit(solution)/shard_map/ppermute | solution.py:18
  567.9 25.1 %collective-permute-start.16 = (f32[8,3,1,128]{3,2,0,1:T(1,128)S(1)}, f32[8,3,1,128]{3,2,0,1:T(1,128)S(1)}, u32[]{:S(2)}, u32[]{:S(2)}) collective-permute-start(f32[8,3,1,128]{3,2,0,1:T(1,128)S(1)} %get-tuple-element.73), channel_id=1, source_target_pairs={{0,8},{8,16},{16,24},{1,9},{9,17},{17,25},{2,10},{10,18},{18,26},{... | collective-permute-start | bytes 36872 | tf_op jit(solution)/shard_map/ppermute | solution.py:15
  573.4 26.9 %copy-start.25 = (f32[32,40,3]{1,2,0:T(4,128)S(1)}, f32[32,40,3]{1,2,0:T(4,128)}, u32[]{:S(2)}) copy-start(f32[32,40,3]{1,2,0:T(4,128)} %copy-done.24) | copy-start | bytes 46084
  573.5 35.5 %copy-start.23 = (s32[2048]{0:T(1024)S(1)}, s32[2048]{0:T(1024)}, u32[]{:S(2)}) copy-start(s32[2048]{0:T(1024)} %copy-done.22) | copy-start | bytes 24580
  588.6 11.7 %all-to-all-start.8 = ((f32[3,32,40]{2,0,1:T(4,128)}), f32[3,32,40]{2,0,1:T(4,128)S(1)}, u32[]{:S(2)}, u32[]{:S(2)}) async-start(f32[3,32,40]{2,0,1:T(4,128)} %bitcast.286), calls=%async_computation.8 | async-start | bytes 131072 | tf_op jit(solution)/shard_map/all_to_all | solution.py:97
  593.0 23.1 %copy-start.62 = (f32[8,3,1,128]{3,2,0,1:T(1,128)}, f32[8,3,1,128]{3,2,0,1:T(1,128)S(1)}, u32[]{:S(2)}) copy-start(f32[8,3,1,128]{3,2,0,1:T(1,128)S(1)} %collective-permute-done.17) | copy-start | bytes 36868
  593.0 23.1 %copy-start.64 = (f32[8,3,1,128]{3,2,0,1:T(1,128)}, f32[8,3,1,128]{3,2,0,1:T(1,128)S(1)}, u32[]{:S(2)}) copy-start(f32[8,3,1,128]{3,2,0,1:T(1,128)S(1)} %collective-permute-done.16) | copy-start | bytes 36868
  594.0 54.8 %collective-permute-start.19 = (f32[8,3,18,1]{3,2,0,1:T(8,128)}, f32[8,3,18,1]{3,2,0,1:T(8,128)}, u32[]{:S(2)}, u32[]{:S(2)}) collective-permute-start(f32[8,3,18,1]{3,2,0,1:T(8,128)} %get-tuple-element.49), channel_id=1, source_target_pairs={{1,0},{2,1},{3,2},{4,3},{5,4},{6,5},{7,6},{9,8},{10,9},{11,10},{12... | collective-permute-start | bytes 5192 | tf_op jit(solution)/shard_map/ppermute | solution.py:18
  595.3 53.5 %collective-permute-start.18 = (f32[8,3,18,1]{3,2,0,1:T(8,128)}, f32[8,3,18,1]{3,2,0,1:T(8,128)}, u32[]{:S(2)}, u32[]{:S(2)}) collective-permute-start(f32[8,3,18,1]{3,2,0,1:T(8,128)} %get-tuple-element.48), channel_id=1, source_target_pairs={{0,1},{1,2},{2,3},{3,4},{4,5},{5,6},{6,7},{8,9},{9,10},{10,11},{11... | collective-permute-start | bytes 5192 | tf_op jit(solution)/shard_map/ppermute | solution.py:15
  617.1 12.2 %all-to-all-start.9 = ((f32[32,3,1,40]{3,2,1,0:T(1,128)}), f32[32,3,1,40]{3,2,1,0:T(1,128)S(1)}, u32[]{:S(2)}, u32[]{:S(2)}) async-start(f32[32,3,1,40]{3,2,1,0:T(1,128)} %copy.731), calls=%async_computation.9 | async-start | bytes 98304 | tf_op jit(solution)/shard_map/all_to_all | solution.py:103
  630.5 60.7 %copy-start.27 = (f32[8,3,16,128]{3,2,0,1:T(8,128)S(1)}, f32[8,3,16,128]{3,2,0,1:T(8,128)}, u32[]{:S(2)}) copy-start(f32[8,3,16,128]{3,2,0,1:T(8,128)} %copy-done.26) | copy-start | bytes 589828
  630.5 60.7 %copy-start.29 = (f32[8,3,16,128]{3,2,0,1:T(8,128)S(1)}, f32[8,3,16,128]{3,2,0,1:T(8,128)}, u32[]{:S(2)}) copy-start(f32[8,3,16,128]{3,2,0,1:T(8,128)} %copy-done.28) | copy-start | bytes 589828
  630.5 60.7 %copy-start.31 = (f32[8,3,16,128]{3,2,0,1:T(8,128)S(1)}, f32[8,3,16,128]{3,2,0,1:T(8,128)}, u32[]{:S(2)}) copy-start(f32[8,3,16,128]{3,2,0,1:T(8,128)} %copy-done.30) | copy-start | bytes 589828
  630.5 60.7 %copy-start.33 = (f32[8,3,16,128]{3,2,0,1:T(8,128)S(1)}, f32[8,3,16,128]{3,2,0,1:T(8,128)}, u32[]{:S(2)}) copy-start(f32[8,3,16,128]{3,2,0,1:T(8,128)} %copy-done.32) | copy-start | bytes 589828
  630.5 60.7 %copy-start.37 = (f32[8,3,16,128]{3,2,1,0:T(8,128)S(1)}, f32[8,3,16,128]{3,2,1,0:T(8,128)}, u32[]{:S(2)}) copy-start(f32[8,3,16,128]{3,2,1,0:T(8,128)} %param.12) | copy-start | bytes 589828
  643.5 47.8 %copy-start.6 = (bf16[8,3,1,16,128]{4,3,2,1,0:T(8,128)(2,1)S(1)}, bf16[8,3,1,16,128]{4,3,2,1,0:T(8,128)(2,1)}, u32[]{:S(2)}) copy-start(bf16[8,3,1,16,128]{4,3,2,1,0:T(8,128)(2,1)} %copy-done.5) | copy-start | bytes 294916
  643.5 47.8 %copy-start.8 = (bf16[8,3,1,16,128]{4,3,2,1,0:T(8,128)(2,1)S(1)}, bf16[8,3,1,16,128]{4,3,2,1,0:T(8,128)(2,1)}, u32[]{:S(2)}) copy-start(bf16[8,3,1,16,128]{4,3,2,1,0:T(8,128)(2,1)} %copy-done.7) | copy-start | bytes 294916
  643.5 47.8 %copy-start.10 = (bf16[8,3,1,16,128]{4,3,2,1,0:T(8,128)(2,1)S(1)}, bf16[8,3,1,16,128]{4,3,2,1,0:T(8,128)(2,1)}, u32[]{:S(2)}) copy-start(bf16[8,3,1,16,128]{4,3,2,1,0:T(8,128)(2,1)} %copy-done.9) | copy-start | bytes 294916
  691.5 25.7 %collective-permute-start.21 = (f32[8,3,1,128]{3,2,0,1:T(1,128)S(1)}, f32[8,3,1,128]{3,2,0,1:T(1,128)S(1)}, u32[]{:S(2)}, u32[]{:S(2)}) collective-permute-start(f32[8,3,1,128]{3,2,0,1:T(1,128)S(1)} %get-tuple-element.67), channel_id=1, source_target_pairs={{8,0},{16,8},{24,16},{9,1},{17,9},{25,17},{10,2},{18,10},{26,18},{... | collective-permute-start | bytes 36872 | tf_op jit(solution)/shard_map/ppermute | solution.py:18
  692.8 24.4 %collective-permute-start.20 = (f32[8,3,1,128]{3,2,0,1:T(1,128)S(1)}, f32[8,3,1,128]{3,2,0,1:T(1,128)S(1)}, u32[]{:S(2)}, u32[]{:S(2)}) collective-permute-start(f32[8,3,1,128]{3,2,0,1:T(1,128)S(1)} %get-tuple-element.66), channel_id=1, source_target_pairs={{0,8},{8,16},{16,24},{1,9},{9,17},{17,25},{2,10},{10,18},{18,26},{... | collective-permute-start | bytes 36872 | tf_op jit(solution)/shard_map/ppermute | solution.py:15
  712.8 11.8 %all-to-all-start.10 = ((f32[3,32,40]{2,0,1:T(4,128)}), f32[3,32,40]{2,0,1:T(4,128)S(1)}, u32[]{:S(2)}, u32[]{:S(2)}) async-start(f32[3,32,40]{2,0,1:T(4,128)} %bitcast.337), calls=%async_computation.10 | async-start | bytes 131072 | tf_op jit(solution)/shard_map/all_to_all | solution.py:97
  718.1 53.6 %collective-permute-start.23 = (f32[8,3,18,1]{3,2,0,1:T(8,128)}, f32[8,3,18,1]{3,2,0,1:T(8,128)}, u32[]{:S(2)}, u32[]{:S(2)}) collective-permute-start(f32[8,3,18,1]{3,2,0,1:T(8,128)} %get-tuple-element.47), channel_id=1, source_target_pairs={{1,0},{2,1},{3,2},{4,3},{5,4},{6,5},{7,6},{9,8},{10,9},{11,10},{12... | collective-permute-start | bytes 5192 | tf_op jit(solution)/shard_map/ppermute | solution.py:18
  719.4 52.3 %collective-permute-start.22 = (f32[8,3,18,1]{3,2,0,1:T(8,128)}, f32[8,3,18,1]{3,2,0,1:T(8,128)}, u32[]{:S(2)}, u32[]{:S(2)}) collective-permute-start(f32[8,3,18,1]{3,2,0,1:T(8,128)} %get-tuple-element.46), channel_id=1, source_target_pairs={{0,1},{1,2},{2,3},{3,4},{4,5},{5,6},{6,7},{8,9},{9,10},{10,11},{11... | collective-permute-start | bytes 5192 | tf_op jit(solution)/shard_map/ppermute | solution.py:15
  741.2 12.1 %all-to-all-start.11 = ((f32[32,3,1,40]{3,2,1,0:T(1,128)}), f32[32,3,1,40]{3,2,1,0:T(1,128)S(1)}, u32[]{:S(2)}, u32[]{:S(2)}) async-start(f32[32,3,1,40]{3,2,1,0:T(1,128)} %copy.738), calls=%async_computation.11 | async-start | bytes 98304 | tf_op jit(solution)/shard_map/all_to_all | solution.py:103
  (45 other events, 425.2 us)
